TPU v7x, 32 devices: a whole 2x2x4 slice. The times are simulated.
32 devices in a mesh: row: 4 (over z), col: 8 (over y, x, core).
Axes of the slice: x: 2, y: 2, z: 4, core: 2. Of those that a mesh axis runs over, the one named last changes fastest.
Arguments:
- tokens: bfloat16 [512, 8192], P('col', 'row'), may hold values from -6 to 6
- w_gate: bfloat16 [8192, 16384], P('row', 'col'), may hold values from -0.09375 to 0.09375
- w_up: bfloat16 [8192, 16384], P('row', 'col'), may hold values from -0.09375 to 0.09375
- w_down: bfloat16 [16384, 8192], P('col', 'row'), may hold values from -0.0625 to 0.0625
- mask_in: int32 [64, 32], P('col', 'row'), may hold values 0 or 1
- mask_out: int32 [64, 32], P('col', 'row'), may hold values 0 or 1
- out_grad: bfloat16 [512, 8192], P('col', 'row'), may hold values from -6 to 6
Outputs:
- output: bfloat16 [512, 8192], P('col', 'row')
- tokens_grad: bfloat16 [512, 8192], P('col', 'row')
- gate_wgrad: bfloat16 [8192, 16384], P('row', 'col')
- up_wgrad: bfloat16 [8192, 16384], P('row', 'col')
- down_wgrad: bfloat16 [16384, 8192], P('col', 'row')
All inputs are finite; a program needn't handle non-finite values. No bound on the sum of `mask_in` or of `mask_out` on one device may be relied on, other than what follows from the above.
Results may differ from a plain program's by a relative error of at most 0.0049.
Values may be sent and summed in bfloat16 or wider, within the bound.
A program may use at most 128 MiB of HBM per device.

v0:
```python
import jax
import jax.numpy as jnp
from jax import lax
from jax.sharding import PartitionSpec as P

BLOCK = 256


def spread(mask_tile):
    return jnp.repeat(jnp.repeat(mask_tile.T, BLOCK, axis=0), BLOCK, axis=1)


def transposed_right(left, right):
    return lax.dot_general(
        left, right, (((1,), (1,)), ((), ())), preferred_element_type=jnp.float32
    )


def transposed_left(left, right):
    return lax.dot_general(
        left, right, (((0,), (0,)), ((), ())), preferred_element_type=jnp.float32
    )


def local(tokens, w_gate, w_up, w_down, mask_in, mask_out, out_grad):
    keep_in = spread(mask_in).astype(jnp.bfloat16)
    keep_out = spread(mask_out).T.astype(jnp.bfloat16)
    gate_masked = w_gate * keep_in
    up_masked = w_up * keep_in
    down_masked = w_down * keep_out
    hidden_width = w_gate.shape[1]
    x_panel = lax.all_gather(tokens, "col", axis=0, tiled=True)
    row_block = x_panel
    gate_part = jnp.dot(row_block, gate_masked, preferred_element_type=jnp.float32)
    up_part = jnp.dot(row_block, up_masked, preferred_element_type=jnp.float32)
    joined = lax.psum_scatter(
        jnp.concatenate([gate_part, up_part], axis=1), "row", scatter_dimension=0, tiled=True
    )
    gate = joined[:, :hidden_width]
    up = joined[:, hidden_width:]
    sigmoid_gate = jax.nn.sigmoid(gate)
    hidden_share = (gate * sigmoid_gate * up).astype(jnp.bfloat16)
    hidden_full = lax.all_gather(hidden_share, "row", axis=0, tiled=True)
    row_block = hidden_full
    output = lax.psum_scatter(
        jnp.dot(row_block, down_masked, preferred_element_type=jnp.float32),
        "col",
        scatter_dimension=0,
        tiled=True,
    ).astype(jnp.bfloat16)
    dy_panel = lax.all_gather(out_grad, "col", axis=0, tiled=True)
    down_wgrad = (transposed_left(hidden_full, dy_panel) * keep_out.astype(jnp.float32)).astype(
        jnp.bfloat16
    )
    row_block = dy_panel
    hidden_grad = lax.psum_scatter(
        transposed_right(row_block, down_masked), "row", scatter_dimension=0, tiled=True
    )
    up_grad = (hidden_grad * gate * sigmoid_gate).astype(jnp.bfloat16)
    gate_grad = (hidden_grad * up * sigmoid_gate * (1.0 + gate * (1.0 - sigmoid_gate))).astype(
        jnp.bfloat16
    )
    gate_full, up_full = (
        lax.all_gather(gate_grad, "row", axis=0, tiled=True),
        lax.all_gather(up_grad, "row", axis=0, tiled=True),
    )
    keep_wide = keep_in.astype(jnp.float32)
    gate_wgrad = (transposed_left(x_panel, gate_full) * keep_wide).astype(jnp.bfloat16)
    up_wgrad = (transposed_left(x_panel, up_full) * keep_wide).astype(jnp.bfloat16)
    tokens_grad = lax.psum_scatter(
        transposed_right(gate_full, gate_masked) + transposed_right(up_full, up_masked),
        "col",
        scatter_dimension=0,
        tiled=True,
    ).astype(jnp.bfloat16)
    return (output, tokens_grad, gate_wgrad, up_wgrad, down_wgrad)


def solution(mesh):
    placed = (
        P("col", "row"),
        P("row", "col"),
        P("row", "col"),
        P("col", "row"),
        P("col", "row"),
        P("col", "row"),
        P("col", "row"),
    )
    return jax.shard_map(
        local,
        mesh=mesh,
        in_specs=placed,
        out_specs=(
            P("col", "row"),
            P("col", "row"),
            P("row", "col"),
            P("row", "col"),
            P("col", "row"),
        ),
        check_vma=False,
    )
```

profile of v0, /device:TPU:0, one launch (start us, length us, event | category | flops | bytes accessed | tf_op | source)
XLA Modules:
  0.0 554.7 jit_solution(6437327898248120053)
XLA Ops:
  7.2 0.7 all-gather.10.cloned.1.call-update
  7.9 0.7 all-gather.6.cloned.1.call-update
  8.7 0.7 convert_bitcast_fusion
  9.6 7.3 %bitcast_multiply_fusion.2 = bf16[2048,2048]{1,0:T(8,128)(2,1)} fusion(bf16[2048,2048]{1,0:T(8,128)(2,1)} %param.10, bf16[2048,8]{0,1:T(8,128)(2,1)S(1)} %bitcast.48), kind=kLoop, calls=%fused_computation.7 | loop fusion | flops 4194304 | bytes 16809984 | tf_op jit(solution)/shard_map/mul | solution.py:30
  16.9 23.5 %all-gather.10.cloned.1.call-done = bf16[512,2048]{1,0:T(8,128)(2,1)} async-done(((bf16[64,2048]{1,0:T(8,128)(2,1)}), bf16[512,2048]{1,0:T(8,128)(2,1)}) %all-gather.10.cloned.1.call-update) | async-done | bytes 2097168 | tf_op jit(solution)/shard_map/all_gather | solution.py:51
  40.4 10.5 %convolution_bitcast_fusion = f32[512,2048]{0,1:T(8,128)} fusion(bf16[2048,2048]{1,0:T(8,128)(2,1)} %bitcast_multiply_fusion.2, bf16[512,2048]{1,0:T(8,128)(2,1)} %all-gather.10.cloned.1.call-done), kind=kOutput, calls=%fused_computation.9 | convolution fusion | flops 4294967296 | bytes 14680064 | tf_op jit(solution)/shard_map/dot_general | solution.py:14
  51.2 0.4 copy-done.2
  51.7 12.2 %copy.13 = bf16[2048,2048]{0,1:T(8,128)(2,1)} copy(bf16[2048,2048]{1,0:T(8,128)(2,1)} %param.8) | data formatting | bytes 16777216 | tf_op args[1]
  63.9 12.2 %copy.14 = bf16[2048,2048]{0,1:T(8,128)(2,1)} copy(bf16[2048,2048]{1,0:T(8,128)(2,1)} %param.9) | data formatting | bytes 16777216 | tf_op args[2]
  76.2 13.7 %bitcast_multiply_fusion.1 = (bf16[2048,2048]{0,1:T(8,128)(2,1)}, bf16[2048,2048]{0,1:T(8,128)(2,1)}) fusion(bf16[2048,2048]{0,1:T(8,128)(2,1)} %copy.13, bf16[2048,8]{0,1:T(8,128)(2,1)S(1)} %bitcast.50, bf16[2048,2048]{0,1:T(8,128)(2,1)} %copy.14), kind=kLoop, calls=%fused_computation.3 | loop fusion | flops 8388608 | bytes 33587200 | tf_op jit(solution)/shard_map/mul | solution.py:28
  89.9 7.8 %convolution_bitcast_fusion.1 = f32[512,2048]{0,1:T(8,128)S(1)} fusion(bf16[2048,2048]{0,1:T(8,128)(2,1)} %get-tuple-element.14, bf16[512,2048]{1,0:T(8,128)(2,1)} %all-gather.6.cloned.1.call-done), kind=kOutput, calls=%fused_computation.10 | convolution fusion | flops 4294967296 | bytes 14680064 | tf_op jit(solution)/shard_map/dot_general | solution.py:35
  97.7 4.8 convolution_bitcast_fusion.2
  102.5 4.2 pad_maximum_fusion
  106.8 42.4 %reduce-scatter.9.cloned.1.call-done = f32[128,2048]{0,1:T(8,128)} async-done(((f32[512,2048]{0,1:T(8,128)}), f32[128,2048]{0,1:T(8,128)}) %reduce-scatter.9.cloned.1.call-update) | async-done | bytes 1048592 | tf_op jit(solution)/shard_map/reduce_scatter | solution.py:56
  149.2 147.4 %reduce-scatter.5.cloned.1.call-done = f32[128,4096]{0,1:T(8,128)} async-done(((f32[512,4096]{0,1:T(8,128)}), f32[128,4096]{0,1:T(8,128)}) %reduce-scatter.5.cloned.1.call-update) | async-done | bytes 2097168 | tf_op jit(solution)/shard_map/reduce_scatter | solution.py:36
  296.6 3.5 multiply_convert_fusion.1
  300.2 0.5 all-gather.14.cloned.1.call-update
  300.7 0.7 all-gather.8.cloned.1.call-update
  301.7 45.4 %all-gather.12.cloned.1.call-done = bf16[512,2048]{0,1:T(8,128)(2,1)} async-done(((bf16[128,2048]{0,1:T(8,128)(2,1)}), bf16[512,2048]{0,1:T(8,128)(2,1)}) %all-gather.12.cloned.1.call-update) | async-done | bytes 2097168 | tf_op jit(solution)/shard_map/all_gather | solution.py:64
  347.1 10.6 %fusion.3 = f32[512,2048]{1,0:T(8,128)} fusion(bf16[512,2048]{0,1:T(8,128)(2,1)} %all-gather.12.cloned.1.call-done, bf16[2048,2048]{0,1:T(8,128)(2,1)} %get-tuple-element.13), kind=kOutput, calls=%fused_computation.20 | convolution fusion | flops 4294967296 | bytes 14680064 | tf_op jit(solution)/shard_map/dot_general | solution.py:14
  357.7 35.3 %all-gather.14.cloned.1.call-done = bf16[512,2048]{0,1:T(8,128)(2,1)} async-done(((bf16[128,2048]{0,1:T(8,128)(2,1)}), bf16[512,2048]{0,1:T(8,128)(2,1)}) %all-gather.14.cloned.1.call-update) | async-done | bytes 2097168 | tf_op jit(solution)/shard_map/all_gather | solution.py:65
  393.0 11.7 %convolution_add_fusion = f32[512,2048]{1,0:T(8,128)} fusion(f32[512,2048]{1,0:T(8,128)} %fusion.3, bf16[512,2048]{0,1:T(8,128)(2,1)} %all-gather.14.cloned.1.call-done, bf16[2048,2048]{0,1:T(8,128)(2,1)} %get-tuple-element.14), kind=kOutput, calls=%fused_computation.12 | convolution fusion | flops 4296015872 | bytes 18874368 | tf_op jit(solution)/shard_map/dot_general | solution.py:14
  405.1 34.0 %all-gather.8.cloned.1.call-done = bf16[512,2048]{0,1:T(8,128)(2,1)} async-done(((bf16[128,2048]{0,1:T(8,128)(2,1)}), bf16[512,2048]{0,1:T(8,128)(2,1)}) %all-gather.8.cloned.1.call-update) | async-done | bytes 2097168 | tf_op jit(solution)/shard_map/all_gather | solution.py:43
  439.1 10.5 %fusion.2 = f32[512,2048]{1,0:T(8,128)} fusion(bf16[512,2048]{0,1:T(8,128)(2,1)} %all-gather.8.cloned.1.call-done, bf16[2048,2048]{1,0:T(8,128)(2,1)} %bitcast_multiply_fusion.2), kind=kOutput, calls=%fused_computation.19 | convolution fusion | flops 4294967296 | bytes 14680064 | tf_op jit(solution)/shard_map/dot_general | solution.py:46
  449.6 8.5 %fusion = bf16[2048,2048]{0,1:T(8,128)(2,1)} fusion(bf16[512,2048]{0,1:T(8,128)(2,1)} %all-gather.12.cloned.1.call-done, bf16[512,2048]{1,0:T(8,128)(2,1)S(1)} %copy-done.4, bf16[2048,8]{0,1:T(8,128)(2,1)S(1)} %bitcast.51), kind=kOutput, calls=%fused_computation.4 | convolution fusion | flops 4307550208 | bytes 12615680 | tf_op jit(solution)/shard_map/dot_general | solution.py:20
  458.1 12.0 %copy.16 = bf16[2048,2048]{1,0:T(8,128)(2,1)} copy(bf16[2048,2048]{0,1:T(8,128)(2,1)} %fusion) | data formatting | bytes 16777216
  470.1 8.3 %fusion.1 = bf16[2048,2048]{0,1:T(8,128)(2,1)} fusion(bf16[512,2048]{0,1:T(8,128)(2,1)S(1)} %copy-done.1, bf16[512,2048]{1,0:T(8,128)(2,1)} %all-gather.6.cloned.1.call-done, bf16[2048,8]{0,1:T(8,128)(2,1)S(1)} %bitcast.52), kind=kOutput, calls=%fused_computation.5 | convolution fusion | flops 4307550208 | bytes 12615680 | tf_op jit(solution)/shard_map/dot_general | solution.py:20
  478.4 12.4 %copy.17 = bf16[2048,2048]{1,0:T(8,128)(2,1)} copy(bf16[2048,2048]{0,1:T(8,128)(2,1)} %fusion.1) | data formatting | bytes 16777216
  490.8 8.4 %multiply_convert_fusion = bf16[2048,2048]{1,0:T(8,128)(2,1)} fusion(bf16[512,2048]{0,1:T(8,128)(2,1)} %all-gather.8.cloned.1.call-done, bf16[512,2048]{1,0:T(8,128)(2,1)S(1)} %copy-done.3, bf16[2048,8]{0,1:T(8,128)(2,1)S(1)} %bitcast.49), kind=kOutput, calls=%fused_computation.6 | convolution fusion | flops 4307550208 | bytes 12615680 | tf_op jit(solution)/shard_map/dot_general | solution.py:20
  499.2 1.8 convert_element_type.74
  501.0 45.4 %reduce-scatter.7.cloned.1.call-done = f32[64,2048]{1,0:T(8,128)} async-done(((f32[512,2048]{1,0:T(8,128)}), f32[64,2048]{1,0:T(8,128)}) %reduce-scatter.7.cloned.1.call-update) | async-done | bytes 524304 | tf_op jit(solution)/shard_map/reduce_scatter | solution.py:45
  546.4 1.8 convert_element_type.71
  (30 shorter events, 1.4 us)
Async XLA Ops:
  7.2 33.2 %all-gather.10.cloned.1.call-start = ((), (), s32[]{:S(2)}) async-start(), calls=%async_computation.8 | async-start | bytes 2359296 | tf_op jit(solution)/shard_map/all_gather | solution.py:51
  7.9 82.0 %all-gather.6.cloned.1.call-start = ((), (), s32[]{:S(2)}) async-start(), calls=%async_computation.4 | async-start | bytes 2359296 | tf_op jit(solution)/shard_map/all_gather | solution.py:32
  8.7 140.6 %reduce-scatter.9.cloned.1.call-start = ((), (), s32[]{:S(2)}) async-start(), calls=%async_computation.9 | async-start | bytes 5242880 | tf_op jit(solution)/shard_map/reduce_scatter | solution.py:56
  50.9 0.7 copy-start.2
  50.9 245.6 %reduce-scatter.5.cloned.1.call-start = ((), (), s32[]{:S(2)}) async-start(), calls=%async_computation.5 | async-start | bytes 10485760 | tf_op jit(solution)/shard_map/reduce_scatter | solution.py:36
  89.9 7.8 %copy-start = (bf16[2048,2048]{0,1:T(8,128)(2,1)S(1)}, bf16[2048,2048]{0,1:T(8,128)(2,1)}, u32[]{:S(2)}) copy-start(bf16[2048,2048]{0,1:T(8,128)(2,1)} %get-tuple-element.13) | copy-start | bytes 25165828
  89.9 7.8 %copy-start.4 = (bf16[512,2048]{1,0:T(8,128)(2,1)S(1)}, bf16[512,2048]{1,0:T(8,128)(2,1)}, u32[]{:S(2)}) copy-start(bf16[512,2048]{1,0:T(8,128)(2,1)} %all-gather.6.cloned.1.call-done) | copy-start | bytes 6291460
  106.8 240.4 %all-gather.12.cloned.1.call-start = ((), (), s32[]{:S(2)}) async-start(), calls=%async_computation.10 | async-start | bytes 2621440 | tf_op jit(solution)/shard_map/all_gather | solution.py:64
  300.1 92.9 %all-gather.14.cloned.1.call-start = ((), (), s32[]{:S(2)}) async-start(), calls=%async_computation.11 | async-start | bytes 2621440 | tf_op jit(solution)/shard_map/all_gather | solution.py:65
  300.7 138.4 %all-gather.8.cloned.1.call-start = ((), (), s32[]{:S(2)}) async-start(), calls=%async_computation.6 | async-start | bytes 2621440 | tf_op jit(solution)/shard_map/all_gather | solution.py:43
  301.4 197.7 %reduce-scatter.11.cloned.1.call-start = ((), (), s32[]{:S(2)}) async-start(), calls=%async_computation.12 | async-start | bytes 4718592 | tf_op jit(solution)/shard_map/reduce_scatter | solution.py:70
  404.8 141.6 %reduce-scatter.7.cloned.1.call-start = ((), (), s32[]{:S(2)}) async-start(), calls=%async_computation.7 | async-start | bytes 4718592 | tf_op jit(solution)/shard_map/reduce_scatter | solution.py:45
  458.1 12.0 %copy-start.1 = (bf16[512,2048]{0,1:T(8,128)(2,1)S(1)}, bf16[512,2048]{0,1:T(8,128)(2,1)}, u32[]{:S(2)}) copy-start(bf16[512,2048]{0,1:T(8,128)(2,1)} %all-gather.14.cloned.1.call-done) | copy-start | bytes 6291460
  478.4 12.4 %copy-start.3 = (bf16[512,2048]{1,0:T(8,128)(2,1)S(1)}, bf16[512,2048]{1,0:T(8,128)(2,1)}, u32[]{:S(2)}) copy-start(bf16[512,2048]{1,0:T(8,128)(2,1)} %all-gather.10.cloned.1.call-done) | copy-start | bytes 6291460
Sparse Core Ops, SparseCore 0:
  9.9 30.4 all-gather.9
  42.3 27.7 all-gather.5
  72.4 76.7 reduce-scatter.8
  151.4 145.1 reduce-scatter.4
  300.2 46.8 all-gather.11
  348.6 44.4 all-gather.13
  394.6 44.4 all-gather.7
  442.4 49.3 reduce-scatter.10
  495.2 51.1 reduce-scatter.6
where the time goes:
time: 556 us; the launch traced here: 555 us
  waiting for transfers between devices  376 us (68%)
  matrix products  81.1 us (15%)
  local copies, waits for them, and re-layouts  49.6 us (9%)
  other arithmetic  33 us (6%)
  between operations  13.9 us (2%)
    reduce_scatter x1, waiting for transfers between devices, local(): lax.psum_scatter(jnp.concatenate([gate_part, up_part], axis=1), 'row', sc...  147 us
    unnamed x14, local copies, waits for them, and re-layouts  49.3 us
    all_gather x1, waiting for transfers between devices, local(): lax.all_gather(gate_grad, 'row', axis=0, tiled=True)  45.4 us
    reduce_scatter x1, waiting for transfers between devices, local(): lax.psum_scatter(jnp.dot(row_block, down_masked, preferred_element_type=j...  45.4 us
    reduce_scatter x1, waiting for transfers between devices, local(): lax.psum_scatter(transposed_right(row_block, down_masked), 'row', scatter...  42.4 us
    all_gather x1, waiting for transfers between devices, local(): lax.all_gather(up_grad, 'row', axis=0, tiled=True)  35.3 us
    all_gather x1, waiting for transfers between devices, local(): hidden_full = lax.all_gather(hidden_share, 'row', axis=0, tiled=True)  34 us
    dot_general x3, matrix products, transposed_right(): lax.dot_general(left, right, (((1,), (1,)), ((), ())), preferred_element_...  32.8 us
  transfers between devices with their start and end apart: 9, of which 7 were waited for; matrix products, arithmetic and copies ran while one was open for 28% of the time, Pallas kernels for 0%

commit v1 on v0

--- a/solution.py
+++ b/solution.py
@@ -40,7 +40,8 @@
     up = joined[:, hidden_width:]
     sigmoid_gate = jax.nn.sigmoid(gate)
     hidden_share = (gate * sigmoid_gate * up).astype(jnp.bfloat16)
-    hidden_full = lax.all_gather(hidden_share, "row", axis=0, tiled=True)
+    copies = jnp.concatenate([hidden_share] * lax.axis_size("row"), axis=0)
+    hidden_full = lax.all_to_all(copies, "row", 0, 0, tiled=True)
     row_block = hidden_full
     output = lax.psum_scatter(
         jnp.dot(row_block, down_masked, preferred_element_type=jnp.float32),

time: 556 us -> 533 us (0.959)
  waiting for transfers between devices: 376 us -> 297 us
  blocking collectives: 0 us -> 50.9 us
    all_to_all x0 -> x1, blocking collectives: none -> 50.9 us  [local(): hidden_full = lax.all_to_all(copies, 'row', 0, 0, tiled=True)]
    reduce_scatter x1, waiting for transfers between devices: 45.4 us -> 0.01 us  [local(): lax.psum_scatter(jnp.dot(row_block, down_masked, preferred_element_type=j...]
    all_gather x1 -> x0, waiting for transfers between devices: 34 us -> none  [local(): hidden_full = lax.all_gather(hidden_share, 'row', axis=0, tiled=True)]
    unnamed x14 -> x16, local copies, waits for them, and re-layouts: 49.3 us -> 51.5 us
  transfers between devices with their start and end apart: 9 -> 8, of which waited for: 7 -> 5; matrix products, arithmetic and copies ran while one was open for 28% -> 28% of each run, Pallas kernels for 0% -> 0%
where the time goes in v1:
time: 533 us; the launch traced here: 531 us
  waiting for transfers between devices  297 us (56%)
  matrix products  80.8 us (15%)
  local copies, waits for them, and re-layouts  54.5 us (10%)
  blocking collectives  50.9 us (10%)
  other arithmetic  33.2 us (6%)
  between operations  14.2 us (3%)
    reduce_scatter x1, waiting for transfers between devices, local(): lax.psum_scatter(jnp.concatenate([gate_part, up_part], axis=1), 'row', sc...  147 us
    unnamed x16, local copies, waits for them, and re-layouts  51.5 us
    all_to_all x1, blocking collectives, local(): hidden_full = lax.all_to_all(copies, 'row', 0, 0, tiled=True)  50.9 us
    all_gather x1, waiting for transfers between devices, local(): lax.all_gather(gate_grad, 'row', axis=0, tiled=True)  46.2 us
    reduce_scatter x1, waiting for transfers between devices, local(): lax.psum_scatter(transposed_right(row_block, down_masked), 'row', scatter...  42.4 us
    all_gather x1, waiting for transfers between devices, local(): lax.all_gather(up_grad, 'row', axis=0, tiled=True)  35.3 us
    dot_general x3, matrix products, transposed_right(): lax.dot_general(left, right, (((1,), (1,)), ((), ())), preferred_element_...  32.8 us
    dot_general x3, matrix products, transposed_left(): lax.dot_general(left, right, (((0,), (0,)), ((), ())), preferred_element_...  25 us
  transfers between devices with their start and end apart: 8, of which 5 were waited for; matrix products, arithmetic and copies ran while one was open for 28% of the time, Pallas kernels for 0%

profile of v1, /device:TPU:0, one launch (start us, length us, event | category | flops | bytes accessed | tf_op | source)
XLA Modules:
  0.0 531.1 jit_solution(96348326615821059)
XLA Ops:
  7.2 0.7 all-gather.7.cloned.1.call-update
  7.9 0.7 all-gather.5.cloned.1.call-update
  8.7 0.7 convert_bitcast_fusion
  9.6 7.3 %bitcast_multiply_fusion.2 = bf16[2048,2048]{1,0:T(8,128)(2,1)} fusion(bf16[2048,2048]{1,0:T(8,128)(2,1)} %param.10, bf16[2048,8]{0,1:T(8,128)(2,1)S(1)} %bitcast.56), kind=kLoop, calls=%fused_computation.7 | loop fusion | flops 4194304 | bytes 16809984 | tf_op jit(solution)/shard_map/mul | solution.py:30
  16.9 23.5 %all-gather.7.cloned.1.call-done = bf16[512,2048]{1,0:T(8,128)(2,1)} async-done(((bf16[64,2048]{1,0:T(8,128)(2,1)}), bf16[512,2048]{1,0:T(8,128)(2,1)}) %all-gather.7.cloned.1.call-update) | async-done | bytes 2097168 | tf_op jit(solution)/shard_map/all_gather | solution.py:52
  40.4 10.5 %convolution_bitcast_fusion = f32[512,2048]{0,1:T(8,128)} fusion(bf16[2048,2048]{1,0:T(8,128)(2,1)} %bitcast_multiply_fusion.2, bf16[512,2048]{1,0:T(8,128)(2,1)} %all-gather.7.cloned.1.call-done), kind=kOutput, calls=%fused_computation.9 | convolution fusion | flops 4294967296 | bytes 14680064 | tf_op jit(solution)/shard_map/dot_general | solution.py:14
  51.2 0.4 copy-done.3
  51.7 12.2 %copy.26 = bf16[2048,2048]{0,1:T(8,128)(2,1)} copy(bf16[2048,2048]{1,0:T(8,128)(2,1)} %param.8) | data formatting | bytes 16777216 | tf_op args[1]
  63.9 12.2 %copy.27 = bf16[2048,2048]{0,1:T(8,128)(2,1)} copy(bf16[2048,2048]{1,0:T(8,128)(2,1)} %param.9) | data formatting | bytes 16777216 | tf_op args[2]
  76.2 13.7 %bitcast_multiply_fusion.1 = (bf16[2048,2048]{0,1:T(8,128)(2,1)}, bf16[2048,2048]{0,1:T(8,128)(2,1)}) fusion(bf16[2048,2048]{0,1:T(8,128)(2,1)} %copy.26, bf16[2048,8]{0,1:T(8,128)(2,1)S(1)} %bitcast.58, bf16[2048,2048]{0,1:T(8,128)(2,1)} %copy.27), kind=kLoop, calls=%fused_computation.3 | loop fusion | flops 8388608 | bytes 33587200 | tf_op jit(solution)/shard_map/mul | solution.py:28
  89.9 7.8 %convolution_bitcast_fusion.1 = f32[512,2048]{0,1:T(8,128)S(1)} fusion(bf16[2048,2048]{0,1:T(8,128)(2,1)} %get-tuple-element.24, bf16[512,2048]{1,0:T(8,128)(2,1)} %all-gather.5.cloned.1.call-done), kind=kOutput, calls=%fused_computation.10 | convolution fusion | flops 4294967296 | bytes 14680064 | tf_op jit(solution)/shard_map/dot_general | solution.py:35
  97.7 4.8 convolution_bitcast_fusion.2
  102.5 4.2 pad_maximum_fusion
  106.8 42.4 %reduce-scatter.9.cloned.1.call-done = f32[128,2048]{0,1:T(8,128)} async-done(((f32[512,2048]{0,1:T(8,128)}), f32[128,2048]{0,1:T(8,128)}) %reduce-scatter.9.cloned.1.call-update) | async-done | bytes 1048592 | tf_op jit(solution)/shard_map/reduce_scatter | solution.py:57
  149.2 147.4 %reduce-scatter.5.cloned.1.call-done = f32[128,4096]{0,1:T(8,128)} async-done(((f32[512,4096]{0,1:T(8,128)}), f32[128,4096]{0,1:T(8,128)}) %reduce-scatter.5.cloned.1.call-update) | async-done | bytes 2097168 | tf_op jit(solution)/shard_map/reduce_scatter | solution.py:36
  296.6 3.4 multiply_convert_fusion.1
  300.1 0.5 all-gather.11.cloned.1.call-update
  300.9 46.2 %all-gather.9.cloned.1.call-done = bf16[512,2048]{0,1:T(8,128)(2,1)} async-done(((bf16[128,2048]{0,1:T(8,128)(2,1)}), bf16[512,2048]{0,1:T(8,128)(2,1)}) %all-gather.9.cloned.1.call-update) | async-done | bytes 2097168 | tf_op jit(solution)/shard_map/all_gather | solution.py:65
  347.1 10.6 %fusion.3 = f32[512,2048]{1,0:T(8,128)} fusion(bf16[512,2048]{0,1:T(8,128)(2,1)} %all-gather.9.cloned.1.call-done, bf16[2048,2048]{0,1:T(8,128)(2,1)} %get-tuple-element.23), kind=kOutput, calls=%fused_computation.22 | convolution fusion | flops 4294967296 | bytes 14680064 | tf_op jit(solution)/shard_map/dot_general | solution.py:14
  357.6 35.3 %all-gather.11.cloned.1.call-done = bf16[512,2048]{0,1:T(8,128)(2,1)} async-done(((bf16[128,2048]{0,1:T(8,128)(2,1)}), bf16[512,2048]{0,1:T(8,128)(2,1)}) %all-gather.11.cloned.1.call-update) | async-done | bytes 2097168 | tf_op jit(solution)/shard_map/all_gather | solution.py:66
  393.0 11.7 %convolution_add_fusion = f32[512,2048]{1,0:T(8,128)} fusion(f32[512,2048]{1,0:T(8,128)} %fusion.3, bf16[512,2048]{0,1:T(8,128)(2,1)} %all-gather.11.cloned.1.call-done, bf16[2048,2048]{0,1:T(8,128)(2,1)} %get-tuple-element.24), kind=kOutput, calls=%fused_computation.12 | convolution fusion | flops 4296015872 | bytes 18874368 | tf_op jit(solution)/shard_map/dot_general | solution.py:14
  405.0 50.9 %all_to_all.12 = bf16[4,128,2048]{1,2,0:T(8,128)(2,1)S(1)} all-to-all(bf16[4,128,2048]{1,2,0:T(8,128)(2,1)S(1)} %copy_bitcast_fusion), channel_id=1, replica_groups=mesh['row'=4,'col'=8] {'row'}, dimensions={0} | all-to-all | bytes 4194304 | tf_op jit(solution)/shard_map/all_to_all | solution.py:44
  456.0 2.7 copy.29
  458.7 10.5 %fusion.2 = f32[512,2048]{1,0:T(8,128)} fusion(bf16[512,2048]{1,0:T(8,128)(2,1)} %bitcast.54, bf16[2048,2048]{1,0:T(8,128)(2,1)} %bitcast_multiply_fusion.2), kind=kOutput, calls=%fused_computation.21 | convolution fusion | flops 4294967296 | bytes 14680064 | tf_op jit(solution)/shard_map/dot_general | solution.py:47
  469.2 1.6 copy-done.5
  470.7 8.3 %fusion = bf16[2048,2048]{0,1:T(8,128)(2,1)} fusion(bf16[512,2048]{0,1:T(8,128)(2,1)} %all-gather.9.cloned.1.call-done, bf16[512,2048]{1,0:T(8,128)(2,1)S(1)} %copy-done.5, bf16[2048,8]{0,1:T(8,128)(2,1)S(1)} %bitcast.59), kind=kOutput, calls=%fused_computation.4 | convolution fusion | flops 4307550208 | bytes 12615680 | tf_op jit(solution)/shard_map/dot_general | solution.py:20
  479.0 12.5 %copy.31 = bf16[2048,2048]{1,0:T(8,128)(2,1)} copy(bf16[2048,2048]{0,1:T(8,128)(2,1)} %fusion) | data formatting | bytes 16777216
  491.6 8.3 %fusion.1 = bf16[2048,2048]{0,1:T(8,128)(2,1)} fusion(bf16[512,2048]{0,1:T(8,128)(2,1)S(1)} %copy-done.1, bf16[512,2048]{1,0:T(8,128)(2,1)} %all-gather.5.cloned.1.call-done, bf16[2048,8]{0,1:T(8,128)(2,1)S(1)} %bitcast.60), kind=kOutput, calls=%fused_computation.5 | convolution fusion | flops 4307550208 | bytes 12615680 | tf_op jit(solution)/shard_map/dot_general | solution.py:20
  499.9 12.5 %copy.32 = bf16[2048,2048]{1,0:T(8,128)(2,1)} copy(bf16[2048,2048]{0,1:T(8,128)(2,1)} %fusion.1) | data formatting | bytes 16777216
  512.3 8.4 %multiply_convert_fusion = bf16[2048,2048]{1,0:T(8,128)(2,1)} fusion(bf16[512,2048]{1,0:T(8,128)(2,1)S(1)} %bitcast.55, bf16[512,2048]{1,0:T(8,128)(2,1)} %all-gather.7.cloned.1.call-done, bf16[2048,8]{0,1:T(8,128)(2,1)S(1)} %bitcast.57), kind=kOutput, calls=%fused_computation.6 | convolution fusion | flops 4307550208 | bytes 12615680 | tf_op jit(solution)/shard_map/dot_general | solution.py:20
  520.7 1.8 convert_element_type.74
  522.5 1.8 convert_element_type.71
  (32 shorter events, 1.4 us)
Async XLA Ops:
  7.2 33.2 %all-gather.7.cloned.1.call-start = ((), (), s32[]{:S(2)}) async-start(), calls=%async_computation.8 | async-start | bytes 2359296 | tf_op jit(solution)/shard_map/all_gather | solution.py:52
  7.9 82.0 %all-gather.5.cloned.1.call-start = ((), (), s32[]{:S(2)}) async-start(), calls=%async_computation.5 | async-start | bytes 2359296 | tf_op jit(solution)/shard_map/all_gather | solution.py:32
  8.7 140.6 %reduce-scatter.9.cloned.1.call-start = ((), (), s32[]{:S(2)}) async-start(), calls=%async_computation.9 | async-start | bytes 5242880 | tf_op jit(solution)/shard_map/reduce_scatter | solution.py:57
  50.9 0.7 copy-start.3
  50.9 245.7 %reduce-scatter.5.cloned.1.call-start = ((), (), s32[]{:S(2)}) async-start(), calls=%async_computation.6 | async-start | bytes 10485760 | tf_op jit(solution)/shard_map/reduce_scatter | solution.py:36
  89.9 7.8 %copy-start = (bf16[2048,2048]{0,1:T(8,128)(2,1)S(1)}, bf16[2048,2048]{0,1:T(8,128)(2,1)}, u32[]{:S(2)}) copy-start(bf16[2048,2048]{0,1:T(8,128)(2,1)} %get-tuple-element.23) | copy-start | bytes 25165828
  89.9 7.8 %copy-start.4 = (bf16[512,2048]{1,0:T(8,128)(2,1)S(1)}, bf16[512,2048]{1,0:T(8,128)(2,1)}, u32[]{:S(2)}) copy-start(bf16[512,2048]{1,0:T(8,128)(2,1)} %all-gather.5.cloned.1.call-done) | copy-start | bytes 6291460
  106.7 240.3 %all-gather.9.cloned.1.call-start = ((), (), s32[]{:S(2)}) async-start(), calls=%async_computation.10 | async-start | bytes 2621440 | tf_op jit(solution)/shard_map/all_gather | solution.py:65
  300.1 92.9 %all-gather.11.cloned.1.call-start = ((), (), s32[]{:S(2)}) async-start(), calls=%async_computation.11 | async-start | bytes 2621440 | tf_op jit(solution)/shard_map/all_gather | solution.py:66
  300.6 220.1 %reduce-scatter.11.cloned.1.call-start = ((), (), s32[]{:S(2)}) async-start(), calls=%async_computation.12 | async-start | bytes 4718592 | tf_op jit(solution)/shard_map/reduce_scatter | solution.py:71
  404.7 117.8 %reduce-scatter.7.cloned.1.call-start = ((), (), s32[]{:S(2)}) async-start(), calls=%async_computation.7 | async-start | bytes 4718592 | tf_op jit(solution)/shard_map/reduce_scatter | solution.py:46
  469.1 1.6 copy-start.5
  479.0 12.5 %copy-start.1 = (bf16[512,2048]{0,1:T(8,128)(2,1)S(1)}, bf16[512,2048]{0,1:T(8,128)(2,1)}, u32[]{:S(2)}) copy-start(bf16[512,2048]{0,1:T(8,128)(2,1)} %all-gather.11.cloned.1.call-done) | copy-start | bytes 6291460
  499.9 12.5 %copy-start.2 = (bf16[4,128,2048]{2,1,0:T(8,128)(2,1)S(1)}, bf16[4,128,2048]{2,1,0:T(8,128)(2,1)}, u32[]{:S(2)}) copy-start(bf16[4,128,2048]{2,1,0:T(8,128)(2,1)} %copy.29) | copy-start | bytes 6291460
Sparse Core Ops, SparseCore 0:
  9.9 30.4 all-gather.6
  42.3 27.7 all-gather.4
  72.4 76.7 reduce-scatter.8
  151.4 145.1 reduce-scatter.4
  300.2 46.8 all-gather.8
  348.5 44.4 all-gather.10
  404.8 49.3 reduce-scatter.10
  469.3 50.2 reduce-scatter.6
